TPU v7x, 32 devices: a whole 2x2x4 slice. The times are simulated.
32 devices in a mesh: phi: 2 (over y), row: 4 (over z), gz: 4 (over x, core).
Axes of the slice: x: 2, y: 2, z: 4, core: 2. Of those that a mesh axis runs over, the one named last changes fastest.
Arguments:
- density: float32 [16, 64, 512], P('phi', 'row', 'gz'), may hold values from -6 to 6
- drift_speed: float32 [3, 64, 512], P(None, 'row', 'gz'), may hold values from -0.5 to 0.5
- viscosity: float32 [64, 512], P('row', 'gz'), may hold values from 0.02 to 0.12
- offsets: int32 [64], P('row'), may hold values from 0 to 15, as said below
Outputs:
- evolved: float32 [16, 64, 512], P('phi', 'row', 'gz')
Inputs may be any that keep to these rules, and one draw needn't show every extreme that they name: `offsets`: both 0 and 15 occur.
All inputs are finite; a program needn't handle non-finite values.
Results may differ from a plain program's by a relative error of at most 0.00002.
Values sent between devices are 32-bit elements; how exact they have to be, the bound alone decides.
A program may use at most 64 MiB of HBM per device.

v0:
```python
import jax
import jax.numpy as jnp
from jax import lax
from jax.sharding import PartitionSpec as P

STEPS = 2


def padded_2(block, sides, width):
    for axis, dim in sides:
        count = lax.axis_size(axis)
        forward = [(i, i + 1) for i in range(count - 1)]
        forward.append((count - 1, 0))
        backward = [(target, source) for source, target in forward]
        low = lax.ppermute(
            lax.slice_in_dim(block, block.shape[dim] - width, None, axis=dim), axis, forward
        )
        high = lax.ppermute(lax.slice_in_dim(block, 0, width, axis=dim), axis, backward)
        block = jnp.concatenate([low, block, high], axis=dim)
    return block


def shifted(block, axis, distance):
    devices = range(lax.axis_size(axis))
    route = [((i - distance) % len(devices), i) for i in devices]
    return lax.ppermute(block, axis, route)


def difference(ahead_one, behind_one, ahead_two, behind_two):
    return (8.0 * (ahead_one - behind_one) - (ahead_two - behind_two)) / 12.0


def tendency(padded, drift_speed, viscosity):
    centre = padded[2:-2, 2:-2, 2:-2]
    phi_ahead = padded[3:-1, 2:-2, 2:-2]
    phi_behind = padded[1:-3, 2:-2, 2:-2]
    rad_ahead = padded[2:-2, 3:-1, 2:-2]
    rad_behind = padded[2:-2, 1:-3, 2:-2]
    hgt_ahead = padded[2:-2, 2:-2, 3:-1]
    hgt_behind = padded[2:-2, 2:-2, 1:-3]
    phi_slope = difference(phi_ahead, phi_behind, padded[4:, 2:-2, 2:-2], padded[:-4, 2:-2, 2:-2])
    rad_slope = difference(rad_ahead, rad_behind, padded[2:-2, 4:, 2:-2], padded[2:-2, :-4, 2:-2])
    hgt_slope = difference(hgt_ahead, hgt_behind, padded[2:-2, 2:-2, 4:], padded[2:-2, 2:-2, :-4])
    neighbours = phi_ahead + phi_behind + rad_ahead + rad_behind + hgt_ahead + hgt_behind
    transport = drift_speed[0] * phi_slope + drift_speed[1] * rad_slope + drift_speed[2] * hgt_slope
    return -transport + viscosity * (neighbours - 6.0 * centre)


def zero_outside(values, margin, rad_local, hgt_local):
    rad_index = (
        lax.axis_index("row") * rad_local + jnp.arange(values.shape[1], dtype=jnp.int32) - margin
    )
    hgt_index = (
        lax.axis_index("gz") * hgt_local + jnp.arange(values.shape[2], dtype=jnp.int32) - margin
    )
    rad_inside = (rad_index >= 0) & (rad_index < rad_local * lax.axis_size("row"))
    hgt_inside = (hgt_index >= 0) & (hgt_index < hgt_local * lax.axis_size("gz"))
    inside = rad_inside[:, None] & hgt_inside[None, :]
    return jnp.where(inside[None], values, 0.0)


def crop_box(values, width):
    return values[
        width : values.shape[0] - width,
        width : values.shape[1] - width,
        width : values.shape[2] - width,
    ]


def sections_deep(state, drift_speed, viscosity, deep_drift, deep_visc):
    rad_local = state.shape[1]
    hgt_local = state.shape[2]
    grown = padded_2(state, (("phi", 0), ("row", 1), ("gz", 2)), 6)
    extended = zero_outside(grown, 6, rad_local, hgt_local)
    section_one = crop_box(extended, 2) + tendency(
        extended, deep_drift[:, 2:-2, 2:-2], deep_visc[2:-2, 2:-2]
    )
    section_one = zero_outside(section_one, 4, rad_local, hgt_local)
    section_two = 0.75 * crop_box(extended, 4) + 0.25 * (
        crop_box(section_one, 2)
        + tendency(section_one, deep_drift[:, 4:-4, 4:-4], deep_visc[4:-4, 4:-4])
    )
    section_two = zero_outside(section_two, 2, rad_local, hgt_local)
    return crop_box(extended, 6) / 3.0 + 2.0 / 3.0 * (
        crop_box(section_two, 2) + tendency(section_two, drift_speed, viscosity)
    )


def rotate_bits(state, offsets):
    phi_local = state.shape[0]
    whole_turns = offsets // phi_local
    remainder = offsets % phi_local
    previous = shifted(state, "phi", 1)
    joined = jnp.concatenate([previous, state], axis=0)
    span = 1
    while span < phi_local:
        lowered = jnp.concatenate([jnp.zeros_like(joined[:span]), joined[:-span]], axis=0)
        chosen_bit = remainder // span % 2 == 1
        joined = jnp.where(chosen_bit[None, :, None], lowered, joined)
        span = span * 2
    moved = joined[phi_local:]
    for level in range(lax.axis_size("phi").bit_length() - 1):
        turned = shifted(moved, "phi", 2**level)
        chosen = whole_turns // 2**level % 2 == 1
        moved = jnp.where(chosen[None, :, None], turned, moved)
    return moved


def local(density, drift_speed, viscosity, offsets):
    state = density
    coefficients = jnp.concatenate([drift_speed, viscosity[None]], axis=0)
    rim_coeffs = padded_2(coefficients, (("row", 1), ("gz", 2)), 6)
    deep_drift = rim_coeffs[:3]
    deep_visc = rim_coeffs[3]
    for step_index in range(STEPS):
        advanced = sections_deep(state, drift_speed, viscosity, deep_drift, deep_visc)
        state = rotate_bits(advanced, offsets)
    return state


def solution(mesh):
    in_specs = (P("phi", "row", "gz"), P(None, "row", "gz"), P("row", "gz"), P("row"))
    out_specs = P("phi", "row", "gz")
    return jax.shard_map(local, mesh=mesh, in_specs=in_specs, out_specs=out_specs, check_vma=False)
```

profile of v0, /device:TPU:0, one launch (start us, length us, event | category | flops | bytes accessed | tf_op | source)
XLA Modules:
  0.0 76.8 jit_solution(18184521274234503656)
XLA Ops:
  0.0 0.8 %fusion.88 = (f32[4,6,128]{2,1,0:T(8,128)S(1)}, f32[4,6,128]{2,1,0:T(8,128)S(1)}) fusion(f32[3,16,128]{2,1,0:T(8,128)} %param.5, f32[1,16,128]{2,1,0:T(8,128)} %bitcast.21), kind=kLoop, calls=%fused_computation.138 | loop fusion | flops 6144 | bytes 57344 | tf_op jit(solution)/shard_map/concatenate | solution.py:111
  0.8 3.0 %collective-permute-start.6 = (f32[4,6,128]{2,1,0:T(8,128)S(1)}, f32[4,6,128]{2,1,0:T(8,128)S(1)}, u32[]{:S(2)}, u32[]{:S(2)}) collective-permute-start(f32[4,6,128]{2,1,0:T(8,128)S(1)} %get-tuple-element.27), channel_id=1, source_target_pairs={{0,4},{4,8},{8,12},{12,0},{1,5},{5,9},{9,13},{13,1},{2,6},{6,10},{... | collective-permute-start | bytes 36872 | tf_op jit(solution)/shard_map/ppermute | solution.py:15
  3.8 2.1 %collective-permute-start.7 = (f32[4,6,128]{2,1,0:T(8,128)S(1)}, f32[4,6,128]{2,1,0:T(8,128)S(1)}, u32[]{:S(2)}, u32[]{:S(2)}) collective-permute-start(f32[4,6,128]{2,1,0:T(8,128)S(1)} %get-tuple-element.28), channel_id=1, source_target_pairs={{4,0},{8,4},{12,8},{0,12},{5,1},{9,5},{13,9},{1,13},{6,2},{10,6},{... | collective-permute-start | bytes 36872 | tf_op jit(solution)/shard_map/ppermute | solution.py:18
  5.9 1.8 %collective-permute-start.1 = (f32[6,16,128]{2,1,0:T(8,128)S(1)}, f32[6,16,128]{2,1,0:T(8,128)S(1)}, u32[]{:S(2)}, u32[]{:S(2)}) collective-permute-start(f32[6,16,128]{2,1,0:T(8,128)S(1)} %get-tuple-element.25), channel_id=1, source_target_pairs={{16,0},{0,16},{17,1},{1,17},{18,2},{2,18},{19,3},{3,19},{20,4},{4,... | collective-permute-start | bytes 147464 | tf_op jit(solution)/shard_map/ppermute | solution.py:18
  9.0 1.7 %collective-permute-start.9 = (f32[4,28,6]{2,1,0:T(8,128)S(1)}, f32[4,28,6]{2,1,0:T(8,128)S(1)}, u32[]{:S(2)}, u32[]{:S(2)}) collective-permute-start(f32[4,28,6]{2,1,0:T(8,128)S(1)} %get-tuple-element.24), channel_id=1, source_target_pairs={{1,0},{2,1},{3,2},{0,3},{5,4},{6,5},{7,6},{4,7},{9,8},{10,9},{11,1... | collective-permute-start | bytes 8072 | tf_op jit(solution)/shard_map/ppermute | solution.py:18
  10.8 1.9 %collective-permute-done.8 = f32[4,28,6]{2,1,0:T(8,128)S(1)} collective-permute-done((f32[4,28,6]{2,1,0:T(8,128)S(1)}, f32[4,28,6]{2,1,0:T(8,128)S(1)}, u32[]{:S(2)}, u32[]{:S(2)}) %collective-permute-start.8) | collective-permute-done | bytes 2720 | tf_op jit(solution)/shard_map/ppermute | solution.py:15
  13.3 3.6 %collective-permute-start.3 = (f32[20,6,128]{2,1,0:T(8,128)S(1)}, f32[20,6,128]{2,1,0:T(8,128)S(1)}, u32[]{:S(2)}, u32[]{:S(2)}) collective-permute-start(f32[20,6,128]{2,1,0:T(8,128)S(1)} %get-tuple-element.14), channel_id=1, source_target_pairs={{4,0},{8,4},{12,8},{0,12},{5,1},{9,5},{13,9},{1,13},{6,2},{10,6},{... | collective-permute-start | bytes 184328 | tf_op jit(solution)/shard_map/ppermute | solution.py:18
  17.0 2.6 %collective-permute-done.2 = f32[20,6,128]{2,1,0:T(8,128)S(1)} collective-permute-done((f32[20,6,128]{2,1,0:T(8,128)S(1)}, f32[20,6,128]{2,1,0:T(8,128)S(1)}, u32[]{:S(2)}, u32[]{:S(2)}) %collective-permute-start.2) | collective-permute-done | bytes 61472 | tf_op jit(solution)/shard_map/ppermute | solution.py:15
  19.8 1.3 %collective-permute-start.4 = (f32[20,28,6]{2,1,0:T(8,128)S(1)}, f32[20,28,6]{2,1,0:T(8,128)S(1)}, u32[]{:S(2)}, u32[]{:S(2)}) collective-permute-start(f32[20,28,6]{2,1,0:T(8,128)S(1)} %get-tuple-element.9), channel_id=1, source_target_pairs={{0,1},{1,2},{2,3},{3,0},{4,5},{5,6},{6,7},{7,4},{8,9},{9,10},{10,1... | collective-permute-start | bytes 40328 | tf_op jit(solution)/shard_map/ppermute | solution.py:15
  21.8 5.4 %collective-permute-done.4 = f32[20,28,6]{2,1,0:T(8,128)S(1)} collective-permute-done((f32[20,28,6]{2,1,0:T(8,128)S(1)}, f32[20,28,6]{2,1,0:T(8,128)S(1)}, u32[]{:S(2)}, u32[]{:S(2)}) %collective-permute-start.4) | collective-permute-done | bytes 13472 | tf_op jit(solution)/shard_map/ppermute | solution.py:15
  27.1 2.5 %collective-permute-done.5 = f32[20,28,6]{2,1,0:T(8,128)S(1)} collective-permute-done((f32[20,28,6]{2,1,0:T(8,128)S(1)}, f32[20,28,6]{2,1,0:T(8,128)S(1)}, u32[]{:S(2)}, u32[]{:S(2)}) %collective-permute-start.5) | collective-permute-done | bytes 13472 | tf_op jit(solution)/shard_map/ppermute | solution.py:18
  30.1 1.3 %fusion.18 = f32[16,24,136]{2,1,0:T(8,128)S(1)} fusion(f32[20,28,140]{2,1,0:T(8,128)S(1)} %maximum_select_fusion, f32[24,136]{1,0:T(8,128)S(1)} %slice.529, f32[24,136]{1,0:T(8,128)S(1)} %get-tuple-element.19, f32[24,136]{1,0:T(8,128)S(1)} %get-tuple-element.20, f32[24,136]{1,0:T(8,128)S(1)} %get-tuple-element.18, pred[24,136]{1,0:T(8,128)(4,1)S(1)} %broadcast_and_fusion.1), kind=kLoop, calls=%fused_computation.24 | loop fusion | flops 1514496 | bytes 2980032 | tf_op jit(solution)/shard_map/jit(_where)/select_n | solution.py:59
  31.4 1.1 %fusion.46 = f32[12,20,132]{2,1,0:T(8,128)S(1)} fusion(f32[16,24,136]{2,1,0:T(8,128)S(1)} %fusion.18, f32[20,28,140]{2,1,0:T(8,128)S(1)} %maximum_select_fusion, f32[20,132]{1,0:T(8,128)S(1)} %slice.546, f32[20,132]{1,0:T(8,128)S(1)} %get-tuple-element.16, f32[20,132]{1,0:T(8,128)S(1)} %get-tuple-element.17, f32[20,132]{1,0:T(8,128)S(1)} %get-tuple-element.15, ...), kind=kLoop, calls=%fused_computation.61 | loop fusion | flops 1013760 | bytes 1945680 | tf_op jit(solution)/shard_map/jit(_where)/select_n | solution.py:59
  32.8 1.6 %collective-permute-start.10 = (f32[8,16,128]{2,1,0:T(8,128)S(1)}, f32[8,16,128]{2,1,0:T(8,128)S(1)}, u32[]{:S(2)}, u32[]{:S(2)}) collective-permute-start(f32[8,16,128]{2,1,0:T(8,128)S(1)} %fusion.76), channel_id=1, source_target_pairs={{16,0},{0,16},{17,1},{1,17},{18,2},{2,18},{19,3},{3,19},{20,4},{4,... | collective-permute-start | bytes 196616 | tf_op jit(solution)/shard_map/ppermute | solution.py:26
  34.4 2.7 %collective-permute-done.10 = f32[8,16,128]{2,1,0:T(8,128)S(1)} collective-permute-done((f32[8,16,128]{2,1,0:T(8,128)S(1)}, f32[8,16,128]{2,1,0:T(8,128)S(1)}, u32[]{:S(2)}, u32[]{:S(2)}) %collective-permute-start.10) | collective-permute-done | bytes 65568 | tf_op jit(solution)/shard_map/ppermute | solution.py:26
  37.4 1.6 %collective-permute-start.11 = (f32[8,16,128]{2,1,0:T(8,128)S(1)}, f32[8,16,128]{2,1,0:T(8,128)S(1)}, u32[]{:S(2)}, u32[]{:S(2)}) collective-permute-start(f32[8,16,128]{2,1,0:T(8,128)S(1)} %slice_select_fusion.1), channel_id=1, source_target_pairs={{16,0},{0,16},{17,1},{1,17},{18,2},{2,18},{19,3},{3,19},{20,4},{4,... | collective-permute-start | bytes 196616 | tf_op jit(solution)/shard_map/ppermute | solution.py:26
  39.0 2.7 %collective-permute-done.11 = f32[8,16,128]{2,1,0:T(8,128)S(1)} collective-permute-done((f32[8,16,128]{2,1,0:T(8,128)S(1)}, f32[8,16,128]{2,1,0:T(8,128)S(1)}, u32[]{:S(2)}, u32[]{:S(2)}) %collective-permute-start.11) | collective-permute-done | bytes 65568 | tf_op jit(solution)/shard_map/ppermute | solution.py:26
  41.7 1.6 %collective-permute-start.12 = (f32[6,16,128]{2,1,0:T(8,128)S(1)}, f32[6,16,128]{2,1,0:T(8,128)S(1)}, u32[]{:S(2)}, u32[]{:S(2)}) collective-permute-start(f32[6,16,128]{2,1,0:T(8,128)S(1)} %get-tuple-element.21), channel_id=1, source_target_pairs={{0,16},{16,0},{1,17},{17,1},{2,18},{18,2},{3,19},{19,3},{4,20},{20... | collective-permute-start | bytes 147464 | tf_op jit(solution)/shard_map/ppermute | solution.py:15
  43.8 2.1 %collective-permute-done.12 = f32[6,16,128]{2,1,0:T(8,128)S(1)} collective-permute-done((f32[6,16,128]{2,1,0:T(8,128)S(1)}, f32[6,16,128]{2,1,0:T(8,128)S(1)}, u32[]{:S(2)}, u32[]{:S(2)}) %collective-permute-start.12) | collective-permute-done | bytes 49184 | tf_op jit(solution)/shard_map/ppermute | solution.py:15
  45.9 1.6 %collective-permute-done.13 = f32[6,16,128]{2,1,0:T(8,128)S(1)} collective-permute-done((f32[6,16,128]{2,1,0:T(8,128)S(1)}, f32[6,16,128]{2,1,0:T(8,128)S(1)}, u32[]{:S(2)}, u32[]{:S(2)}) %collective-permute-start.13) | collective-permute-done | bytes 49184 | tf_op jit(solution)/shard_map/ppermute | solution.py:18
  47.5 1.4 %collective-permute-start.14 = (f32[20,6,128]{2,1,0:T(8,128)S(1)}, f32[20,6,128]{2,1,0:T(8,128)S(1)}, u32[]{:S(2)}, u32[]{:S(2)}) collective-permute-start(f32[20,6,128]{2,1,0:T(8,128)S(1)} %get-tuple-element.11), channel_id=1, source_target_pairs={{0,4},{4,8},{8,12},{12,0},{1,5},{5,9},{9,13},{13,1},{2,6},{6,10},{... | collective-permute-start | bytes 184328 | tf_op jit(solution)/shard_map/ppermute | solution.py:15
  49.0 2.4 %collective-permute-start.15 = (f32[20,6,128]{2,1,0:T(8,128)S(1)}, f32[20,6,128]{2,1,0:T(8,128)S(1)}, u32[]{:S(2)}, u32[]{:S(2)}) collective-permute-start(f32[20,6,128]{2,1,0:T(8,128)S(1)} %get-tuple-element.12), channel_id=1, source_target_pairs={{4,0},{8,4},{12,8},{0,12},{5,1},{9,5},{13,9},{1,13},{6,2},{10,6},{... | collective-permute-start | bytes 184328 | tf_op jit(solution)/shard_map/ppermute | solution.py:18
  51.4 2.5 %collective-permute-done.14 = f32[20,6,128]{2,1,0:T(8,128)S(1)} collective-permute-done((f32[20,6,128]{2,1,0:T(8,128)S(1)}, f32[20,6,128]{2,1,0:T(8,128)S(1)}, u32[]{:S(2)}, u32[]{:S(2)}) %collective-permute-start.14) | collective-permute-done | bytes 61472 | tf_op jit(solution)/shard_map/ppermute | solution.py:15
  54.6 1.7 %collective-permute-start.17 = (f32[20,28,6]{2,1,0:T(8,128)S(1)}, f32[20,28,6]{2,1,0:T(8,128)S(1)}, u32[]{:S(2)}, u32[]{:S(2)}) collective-permute-start(f32[20,28,6]{2,1,0:T(8,128)S(1)} %get-tuple-element.8), channel_id=1, source_target_pairs={{1,0},{2,1},{3,2},{0,3},{5,4},{6,5},{7,6},{4,7},{9,8},{10,9},{11,1... | collective-permute-start | bytes 40328 | tf_op jit(solution)/shard_map/ppermute | solution.py:18
  56.3 5.9 %collective-permute-done.16 = f32[20,28,6]{2,1,0:T(8,128)S(1)} collective-permute-done((f32[20,28,6]{2,1,0:T(8,128)S(1)}, f32[20,28,6]{2,1,0:T(8,128)S(1)}, u32[]{:S(2)}, u32[]{:S(2)}) %collective-permute-start.16) | collective-permute-done | bytes 13472 | tf_op jit(solution)/shard_map/ppermute | solution.py:15
  62.2 1.8 %collective-permute-done.17 = f32[20,28,6]{2,1,0:T(8,128)S(1)} collective-permute-done((f32[20,28,6]{2,1,0:T(8,128)S(1)}, f32[20,28,6]{2,1,0:T(8,128)S(1)}, u32[]{:S(2)}, u32[]{:S(2)}) %collective-permute-start.17) | collective-permute-done | bytes 13472 | tf_op jit(solution)/shard_map/ppermute | solution.py:18
  64.5 1.3 %fusion.6 = f32[16,24,136]{2,1,0:T(8,128)S(1)} fusion(f32[20,28,140]{2,1,0:T(8,128)S(1)} %maximum_select_fusion.1, f32[24,136]{1,0:T(8,128)S(1)} %slice.529, f32[24,136]{1,0:T(8,128)S(1)} %get-tuple-element.19, f32[24,136]{1,0:T(8,128)S(1)} %get-tuple-element.20, f32[24,136]{1,0:T(8,128)S(1)} %get-tuple-element.18, pred[24,136]{1,0:T(8,128)(4,1)S(1)} %broadcast_and_fusion.1), kind=kLoop, calls=%fused_computation.9 | loop fusion | flops 1514496 | bytes 2980032 | tf_op jit(solution)/shard_map/jit(_where)/select_n | solution.py:59
  65.8 1.1 %fusion.32 = f32[12,20,132]{2,1,0:T(8,128)S(1)} fusion(f32[16,24,136]{2,1,0:T(8,128)S(1)} %fusion.6, f32[20,28,140]{2,1,0:T(8,128)S(1)} %maximum_select_fusion.1, f32[20,132]{1,0:T(8,128)S(1)} %slice.546, f32[20,132]{1,0:T(8,128)S(1)} %get-tuple-element.16, f32[20,132]{1,0:T(8,128)S(1)} %get-tuple-element.17, f32[20,132]{1,0:T(8,128)S(1)} %get-tuple-element.15, ...), kind=kLoop, calls=%fused_computation.43 | loop fusion | flops 1013760 | bytes 1945680 | tf_op jit(solution)/shard_map/jit(_where)/select_n | solution.py:59
  67.1 0.7 collective-permute-start.18
  67.8 3.7 %collective-permute-done.18 = f32[8,16,128]{2,1,0:T(8,128)S(1)} collective-permute-done((f32[8,16,128]{2,1,0:T(8,128)S(1)}, f32[8,16,128]{2,1,0:T(8,128)S(1)}, u32[]{:S(2)}, u32[]{:S(2)}) %collective-permute-start.18) | collective-permute-done | bytes 65568 | tf_op jit(solution)/shard_map/ppermute | solution.py:26
  72.4 3.7 %collective-permute-done.19 = f32[8,16,128]{2,1,0:T(8,128)S(1)} collective-permute-done((f32[8,16,128]{2,1,0:T(8,128)S(1)}, f32[8,16,128]{2,1,0:T(8,128)S(1)}, u32[]{:S(2)}, u32[]{:S(2)}) %collective-permute-start.19) | collective-permute-done | bytes 65568 | tf_op jit(solution)/shard_map/ppermute | solution.py:26
  76.1 0.7 broadcast_select_fusion
  (71 shorter events, 6.6 us)
Async XLA Ops:
  0.0 5.9 %copy-start = (f32[8,16,128]{2,1,0:T(8,128)S(1)}, f32[8,16,128]{2,1,0:T(8,128)}, u32[]{:S(2)}) copy-start(f32[8,16,128]{2,1,0:T(8,128)} %param.4) | copy-start | bytes 196612
  0.8 7.6 %collective-permute-start.6 = (f32[4,6,128]{2,1,0:T(8,128)S(1)}, f32[4,6,128]{2,1,0:T(8,128)S(1)}, u32[]{:S(2)}, u32[]{:S(2)}) collective-permute-start(f32[4,6,128]{2,1,0:T(8,128)S(1)} %get-tuple-element.27), channel_id=1, source_target_pairs={{0,4},{4,8},{8,12},{12,0},{1,5},{5,9},{9,13},{13,1},{2,6},{6,10},{... | collective-permute-start | bytes 36872 | tf_op jit(solution)/shard_map/ppermute | solution.py:15
  3.8 4.5 %collective-permute-start.7 = (f32[4,6,128]{2,1,0:T(8,128)S(1)}, f32[4,6,128]{2,1,0:T(8,128)S(1)}, u32[]{:S(2)}, u32[]{:S(2)}) collective-permute-start(f32[4,6,128]{2,1,0:T(8,128)S(1)} %get-tuple-element.28), channel_id=1, source_target_pairs={{4,0},{8,4},{12,8},{0,12},{5,1},{9,5},{13,9},{1,13},{6,2},{10,6},{... | collective-permute-start | bytes 36872 | tf_op jit(solution)/shard_map/ppermute | solution.py:18
  5.9 2.2 %copy-start.1 = (f32[3,16,128]{2,1,0:T(8,128)S(1)}, f32[3,16,128]{2,1,0:T(8,128)}, u32[]{:S(2)}) copy-start(f32[3,16,128]{2,1,0:T(8,128)} %param.5) | copy-start | bytes 73732
  5.9 7.1 %collective-permute-start.1 = (f32[6,16,128]{2,1,0:T(8,128)S(1)}, f32[6,16,128]{2,1,0:T(8,128)S(1)}, u32[]{:S(2)}, u32[]{:S(2)}) collective-permute-start(f32[6,16,128]{2,1,0:T(8,128)S(1)} %get-tuple-element.25), channel_id=1, source_target_pairs={{16,0},{0,16},{17,1},{1,17},{18,2},{2,18},{19,3},{3,19},{20,4},{4,... | collective-permute-start | bytes 147464 | tf_op jit(solution)/shard_map/ppermute | solution.py:18
  7.7 5.3 %collective-permute-start = (f32[6,16,128]{2,1,0:T(8,128)S(1)}, f32[6,16,128]{2,1,0:T(8,128)S(1)}, u32[]{:S(2)}, u32[]{:S(2)}) collective-permute-start(f32[6,16,128]{2,1,0:T(8,128)S(1)} %get-tuple-element.26), channel_id=1, source_target_pairs={{0,16},{16,0},{1,17},{17,1},{2,18},{18,2},{3,19},{19,3},{4,20},{20... | collective-permute-start | bytes 147464 | tf_op jit(solution)/shard_map/ppermute | solution.py:15
  8.2 0.7 copy-start.2
  9.0 1.8 %copy-start.3 = (s32[16]{0:T(128)S(1)}, s32[16]{0:T(128)}, u32[]{:S(2)}) copy-start(s32[16]{0:T(128)} %param.7) | copy-start | bytes 196
  9.0 3.7 %collective-permute-start.8 = (f32[4,28,6]{2,1,0:T(8,128)S(1)}, f32[4,28,6]{2,1,0:T(8,128)S(1)}, u32[]{:S(2)}, u32[]{:S(2)}) collective-permute-start(f32[4,28,6]{2,1,0:T(8,128)S(1)} %get-tuple-element.23), channel_id=1, source_target_pairs={{0,1},{1,2},{2,3},{3,0},{4,5},{5,6},{6,7},{7,4},{8,9},{9,10},{10,1... | collective-permute-start | bytes 8072 | tf_op jit(solution)/shard_map/ppermute | solution.py:15
  9.0 3.7 %collective-permute-start.9 = (f32[4,28,6]{2,1,0:T(8,128)S(1)}, f32[4,28,6]{2,1,0:T(8,128)S(1)}, u32[]{:S(2)}, u32[]{:S(2)}) collective-permute-start(f32[4,28,6]{2,1,0:T(8,128)S(1)} %get-tuple-element.24), channel_id=1, source_target_pairs={{1,0},{2,1},{3,2},{0,3},{5,4},{6,5},{7,6},{4,7},{9,8},{10,9},{11,1... | collective-permute-start | bytes 8072 | tf_op jit(solution)/shard_map/ppermute | solution.py:18
  13.0 6.5 %collective-permute-start.2 = (f32[20,6,128]{2,1,0:T(8,128)S(1)}, f32[20,6,128]{2,1,0:T(8,128)S(1)}, u32[]{:S(2)}, u32[]{:S(2)}) collective-permute-start(f32[20,6,128]{2,1,0:T(8,128)S(1)} %get-tuple-element.13), channel_id=1, source_target_pairs={{0,4},{4,8},{8,12},{12,0},{1,5},{5,9},{9,13},{13,1},{2,6},{6,10},{... | collective-permute-start | bytes 184328 | tf_op jit(solution)/shard_map/ppermute | solution.py:15
  13.3 6.2 %collective-permute-start.3 = (f32[20,6,128]{2,1,0:T(8,128)S(1)}, f32[20,6,128]{2,1,0:T(8,128)S(1)}, u32[]{:S(2)}, u32[]{:S(2)}) collective-permute-start(f32[20,6,128]{2,1,0:T(8,128)S(1)} %get-tuple-element.14), channel_id=1, source_target_pairs={{4,0},{8,4},{12,8},{0,12},{5,1},{9,5},{13,9},{1,13},{6,2},{10,6},{... | collective-permute-start | bytes 184328 | tf_op jit(solution)/shard_map/ppermute | solution.py:18
  19.8 7.3 %collective-permute-start.4 = (f32[20,28,6]{2,1,0:T(8,128)S(1)}, f32[20,28,6]{2,1,0:T(8,128)S(1)}, u32[]{:S(2)}, u32[]{:S(2)}) collective-permute-start(f32[20,28,6]{2,1,0:T(8,128)S(1)} %get-tuple-element.9), channel_id=1, source_target_pairs={{0,1},{1,2},{2,3},{3,0},{4,5},{5,6},{6,7},{7,4},{8,9},{9,10},{10,1... | collective-permute-start | bytes 40328 | tf_op jit(solution)/shard_map/ppermute | solution.py:15
  21.1 8.5 %collective-permute-start.5 = (f32[20,28,6]{2,1,0:T(8,128)S(1)}, f32[20,28,6]{2,1,0:T(8,128)S(1)}, u32[]{:S(2)}, u32[]{:S(2)}) collective-permute-start(f32[20,28,6]{2,1,0:T(8,128)S(1)} %get-tuple-element.10), channel_id=1, source_target_pairs={{1,0},{2,1},{3,2},{0,3},{5,4},{6,5},{7,6},{4,7},{9,8},{10,9},{11,1... | collective-permute-start | bytes 40328 | tf_op jit(solution)/shard_map/ppermute | solution.py:18
  32.8 4.3 %collective-permute-start.10 = (f32[8,16,128]{2,1,0:T(8,128)S(1)}, f32[8,16,128]{2,1,0:T(8,128)S(1)}, u32[]{:S(2)}, u32[]{:S(2)}) collective-permute-start(f32[8,16,128]{2,1,0:T(8,128)S(1)} %fusion.76), channel_id=1, source_target_pairs={{16,0},{0,16},{17,1},{1,17},{18,2},{2,18},{19,3},{3,19},{20,4},{4,... | collective-permute-start | bytes 196616 | tf_op jit(solution)/shard_map/ppermute | solution.py:26
  37.4 4.3 %collective-permute-start.11 = (f32[8,16,128]{2,1,0:T(8,128)S(1)}, f32[8,16,128]{2,1,0:T(8,128)S(1)}, u32[]{:S(2)}, u32[]{:S(2)}) collective-permute-start(f32[8,16,128]{2,1,0:T(8,128)S(1)} %slice_select_fusion.1), channel_id=1, source_target_pairs={{16,0},{0,16},{17,1},{1,17},{18,2},{2,18},{19,3},{3,19},{20,4},{4,... | collective-permute-start | bytes 196616 | tf_op jit(solution)/shard_map/ppermute | solution.py:26
  41.7 4.2 %collective-permute-start.12 = (f32[6,16,128]{2,1,0:T(8,128)S(1)}, f32[6,16,128]{2,1,0:T(8,128)S(1)}, u32[]{:S(2)}, u32[]{:S(2)}) collective-permute-start(f32[6,16,128]{2,1,0:T(8,128)S(1)} %get-tuple-element.21), channel_id=1, source_target_pairs={{0,16},{16,0},{1,17},{17,1},{2,18},{18,2},{3,19},{19,3},{4,20},{20... | collective-permute-start | bytes 147464 | tf_op jit(solution)/shard_map/ppermute | solution.py:15
  43.4 4.1 %collective-permute-start.13 = (f32[6,16,128]{2,1,0:T(8,128)S(1)}, f32[6,16,128]{2,1,0:T(8,128)S(1)}, u32[]{:S(2)}, u32[]{:S(2)}) collective-permute-start(f32[6,16,128]{2,1,0:T(8,128)S(1)} %get-tuple-element.22), channel_id=1, source_target_pairs={{16,0},{0,16},{17,1},{1,17},{18,2},{2,18},{19,3},{3,19},{20,4},{4,... | collective-permute-start | bytes 147464 | tf_op jit(solution)/shard_map/ppermute | solution.py:18
  47.5 6.4 %collective-permute-start.14 = (f32[20,6,128]{2,1,0:T(8,128)S(1)}, f32[20,6,128]{2,1,0:T(8,128)S(1)}, u32[]{:S(2)}, u32[]{:S(2)}) collective-permute-start(f32[20,6,128]{2,1,0:T(8,128)S(1)} %get-tuple-element.11), channel_id=1, source_target_pairs={{0,4},{4,8},{8,12},{12,0},{1,5},{5,9},{9,13},{13,1},{2,6},{6,10},{... | collective-permute-start | bytes 184328 | tf_op jit(solution)/shard_map/ppermute | solution.py:15
  49.0 5.3 %collective-permute-start.15 = (f32[20,6,128]{2,1,0:T(8,128)S(1)}, f32[20,6,128]{2,1,0:T(8,128)S(1)}, u32[]{:S(2)}, u32[]{:S(2)}) collective-permute-start(f32[20,6,128]{2,1,0:T(8,128)S(1)} %get-tuple-element.12), channel_id=1, source_target_pairs={{4,0},{8,4},{12,8},{0,12},{5,1},{9,5},{13,9},{1,13},{6,2},{10,6},{... | collective-permute-start | bytes 184328 | tf_op jit(solution)/shard_map/ppermute | solution.py:18
  54.5 7.7 %collective-permute-start.16 = (f32[20,28,6]{2,1,0:T(8,128)S(1)}, f32[20,28,6]{2,1,0:T(8,128)S(1)}, u32[]{:S(2)}, u32[]{:S(2)}) collective-permute-start(f32[20,28,6]{2,1,0:T(8,128)S(1)} %get-tuple-element.7), channel_id=1, source_target_pairs={{0,1},{1,2},{2,3},{3,0},{4,5},{5,6},{6,7},{7,4},{8,9},{9,10},{10,1... | collective-permute-start | bytes 40328 | tf_op jit(solution)/shard_map/ppermute | solution.py:15
  54.6 9.5 %collective-permute-start.17 = (f32[20,28,6]{2,1,0:T(8,128)S(1)}, f32[20,28,6]{2,1,0:T(8,128)S(1)}, u32[]{:S(2)}, u32[]{:S(2)}) collective-permute-start(f32[20,28,6]{2,1,0:T(8,128)S(1)} %get-tuple-element.8), channel_id=1, source_target_pairs={{1,0},{2,1},{3,2},{0,3},{5,4},{6,5},{7,6},{4,7},{9,8},{10,9},{11,1... | collective-permute-start | bytes 40328 | tf_op jit(solution)/shard_map/ppermute | solution.py:18
  67.1 4.4 %collective-permute-start.18 = (f32[8,16,128]{2,1,0:T(8,128)S(1)}, f32[8,16,128]{2,1,0:T(8,128)S(1)}, u32[]{:S(2)}, u32[]{:S(2)}) collective-permute-start(f32[8,16,128]{2,1,0:T(8,128)S(1)} %fusion.63), channel_id=1, source_target_pairs={{16,0},{0,16},{17,1},{1,17},{18,2},{2,18},{19,3},{3,19},{20,4},{4,... | collective-permute-start | bytes 196616 | tf_op jit(solution)/shard_map/ppermute | solution.py:26
  71.8 4.3 %collective-permute-start.19 = (f32[8,16,128]{2,1,0:T(8,128)S(1)}, f32[8,16,128]{2,1,0:T(8,128)S(1)}, u32[]{:S(2)}, u32[]{:S(2)}) collective-permute-start(f32[8,16,128]{2,1,0:T(8,128)S(1)} %slice_select_fusion), channel_id=1, source_target_pairs={{16,0},{0,16},{17,1},{1,17},{18,2},{2,18},{19,3},{3,19},{20,4},{4,... | collective-permute-start | bytes 196616 | tf_op jit(solution)/shard_map/ppermute | solution.py:26
where the time goes:
time: 77.1 us; the launch traced here: 76.8 us
  waiting for transfers between devices  39.4 us (51%)
  starting transfers between devices  26.9 us (35%)
  other arithmetic  8.93 us (12%)
  local copies, waits for them, and re-layouts  1.21 us (2%)
    ppermute x8, waiting for transfers between devices, padded_2(): lax.ppermute(lax.slice_in_dim(block, block.shape[dim] - width, None, axis...  20.4 us
    ppermute x8, starting transfers between devices, padded_2(): lax.ppermute(lax.slice_in_dim(block, 0, width, axis=dim), axis, backward)  14.2 us
    ppermute x4, waiting for transfers between devices, shifted(): return lax.ppermute(block, axis, route)  12.7 us
    ppermute x8, starting transfers between devices, padded_2(): lax.ppermute(lax.slice_in_dim(block, block.shape[dim] - width, None, axis...  8.18 us
    ppermute x8, waiting for transfers between devices, padded_2(): lax.ppermute(lax.slice_in_dim(block, 0, width, axis=dim), axis, backward)  6.31 us
    select_n x6, other arithmetic, zero_outside(): return jnp.where(inside[None], values, 0.0)  5.54 us
    ppermute x4, starting transfers between devices, shifted(): return lax.ppermute(block, axis, route)  4.51 us
  transfers between devices with their start and end apart: 20, of which 14 were waited for; matrix products, arithmetic and copies ran while one was open for 1% of the time, Pallas kernels for 0%

commit v1 on v0

v1 whole, which is shorter than its diff:
```python
import functools

import jax
import jax.numpy as jnp
from jax import lax
from jax.experimental import pallas as pl
from jax.experimental.pallas import tpu as pltpu
from jax.sharding import PartitionSpec as P

STEPS = 2
LANES = 128
RIM = 16
MESH = pl.DeviceIdType.MESH


def kernel(
    sizes, dens, drift, visc, offs, out,
    tx, rx, rh, cx, rc, ch, rch, ext, one, two, coef, txo, rxo,
    s_main, r_main, s_rim, r_rim, s_coef, r_coef, s_crim, r_crim, s_out, r_out,
):
    n, nrow, ngz = sizes
    pl_local, rows, _ = dens.shape
    width = LANES // n
    tiles = pl_local // n
    planes = tiles + 2
    nphi = n * pl_local
    p, i, j = lax.axis_index("phi"), lax.axis_index("row"), lax.axis_index("gz")
    count = tiles + 1 if n == 2 else planes

    def row_ok(d):
        return (i + d >= 0) & (i + d < nrow)

    def dev(t, d, g):
        row = i if d == 0 else lax.rem(i + d + nrow, nrow)
        col = j if g == 0 else lax.rem(j + g + ngz, ngz)
        return (t, row, col)

    first, last = p == 0, p == n - 1
    has_up, has_down = j + 1 < ngz, j >= 1

    barrier = pltpu.get_barrier_semaphore()

    def greet(ok, target):
        @pl.when(ok)
        def _():
            pl.semaphore_signal(barrier, inc=1, device_id=target, device_id_type=MESH)

    for k in range(n):
        t = lax.rem(p + k, n)
        for d in (-1, 0, 1):
            if k or d:
                greet(row_ok(d), dev(t, d, 0))
            greet(row_ok(d) & first & has_down, dev(t, d, -1))
            greet(row_ok(d) & last & has_up, dev(t, d, 1))

    lane = lax.broadcasted_iota(jnp.int32, (rows, LANES), 1)
    sub = lax.broadcasted_iota(jnp.int32, (rows, LANES), 0)

    def roll(x, by):
        if isinstance(by, int):
            by = by % LANES
            return x if by == 0 else pltpu.roll(x, by, 1)
        return pltpu.roll(x, lax.rem(by + 4 * LANES, LANES), 1)

    for c in range(3):
        cx[c] = drift[c] * (-1.0 / 12.0)
    cx[3] = visc[...]
    plane = jnp.zeros((rows, LANES), jnp.float32)
    for r in range(rows):
        plane = jnp.where(sub == r, offs[r].astype(jnp.float32), plane)
    cx[4] = plane
    low, high = jnp.zeros((rows, LANES), jnp.float32), jnp.zeros((rows, LANES), jnp.float32)
    for c in range(5):
        here = lane // RIM == c
        low = jnp.where(here, roll(cx[c], c * RIM - (LANES - RIM)), low)
        high = jnp.where(here, roll(cx[c], c * RIM), high)
    ch[0] = low
    ch[1] = high

    for t in range(n):
        for m in range(tiles):
            acc = None
            for s in range(n):
                part = roll(dens[m * n + s], s * width - t * width)
                acc = part if acc is None else jnp.where(lane >= s * width, part, acc)
            tx[t, 1 + m] = acc
        low = high = None
        for q in range(pl_local):
            part_l = roll(dens[q], q * RIM - t * width + RIM)
            part_h = roll(dens[q], q * RIM - t * width - width)
            low = part_l if low is None else jnp.where(lane >= q * RIM, part_l, low)
            high = part_h if high is None else jnp.where(lane >= q * RIM, part_h, high)
        near, far = (high, low) if t == 0 else (low, high)
        tx[t, 0] = near
        tx[t, planes - 1] = far

    expected = jnp.int32(0)
    for d in (-1, 0, 1):
        here = row_ok(d).astype(jnp.int32)
        expected += here * (n - (d == 0))
        expected += here * (j + 1 < ngz).astype(jnp.int32)
        expected += here * (j >= 1).astype(jnp.int32)
    pl.semaphore_wait(barrier, expected)

    def main_copy(k, d):
        t = lax.rem(p + k, n)
        return pltpu.make_async_remote_copy(
            src_ref=tx.at[t, pl.ds(0, count)],
            dst_ref=rx.at[p, 1 - d, pl.ds(0, count)],
            send_sem=s_main.at[k, d + 1], recv_sem=r_main.at[p, 1 - d],
            device_id=dev(t, d, 0), device_id_type=MESH,
        )

    def rim_copy(side, d):
        t, g, at = (0, 1, planes - 1) if side == 0 else (n - 1, -1, planes - 1)
        return pltpu.make_async_remote_copy(
            src_ref=tx.at[t, at], dst_ref=rh.at[p, 1 - d],
            send_sem=s_rim.at[side, d + 1], recv_sem=r_rim.at[p, 1 - d],
            device_id=dev(t, d, g), device_id_type=MESH,
        )

    def coef_copy(d):
        return pltpu.make_async_remote_copy(
            src_ref=cx, dst_ref=rc.at[1 - d],
            send_sem=s_coef.at[d + 1], recv_sem=r_coef.at[1 - d],
            device_id=dev(p, d, 0), device_id_type=MESH,
        )

    def crim_copy(side, d):
        g = 1 if side == 0 else -1
        return pltpu.make_async_remote_copy(
            src_ref=ch.at[side], dst_ref=rch.at[1 - d],
            send_sem=s_crim.at[d + 1], recv_sem=r_crim.at[1 - d],
            device_id=dev(p, d, g), device_id_type=MESH,
        )

    sends = []
    for k in list(range(1, n)) + [0]:
        for d in (-1, 1, 0):
            if k or d:
                sends.append((row_ok(d), functools.partial(main_copy, k, d)))
    for d in (-1, 1):
        sends.append((row_ok(d), functools.partial(coef_copy, d)))
    for d in (-1, 1, 0):
        sends.append((row_ok(d) & has_up, functools.partial(rim_copy, 0, d)))
        sends.append((row_ok(d) & has_down, functools.partial(rim_copy, 1, d)))
        sends.append((row_ok(d) & has_up & first, functools.partial(crim_copy, 0, d)))
        sends.append((row_ok(d) & has_down & last, functools.partial(crim_copy, 1, d)))
    for ok, make in sends:
        @pl.when(ok)
        def _():
            make().start()

    def await_copy(ok, dst, sem):
        @pl.when(ok)
        def _():
            pltpu.make_async_copy(dst, dst, sem).wait()

    out_ok = (first & has_down) | (last & has_up)
    row_at = i * rows + sub
    hgt_at = j * LANES + p * width + lane - RIM
    hgt_in = (hgt_at >= 0) & (hgt_at < ngz * LANES)

    def inside(slot):
        at = row_at + (slot - 1) * rows
        return hgt_in & (at >= 0) & (at < nrow * rows)

    low_side, high_side = lane < RIM, lane >= RIM + width
    swap = (low_side & first) | (high_side & last)

    for slot in (1, 0, 2):
        ok = row_ok(slot - 1)
        if slot != 1:
            await_copy(ok, rc.at[slot], r_coef.at[slot])
        await_copy(ok & out_ok, rch.at[slot], r_crim.at[slot])
        base = jnp.where(first, 0, RIM + width)
        for c in range(5):
            body = cx[c] if slot == 1 else rc[slot, c]
            value = jnp.where(
                swap, roll(rch[slot], base - c * RIM), roll(body, RIM - p * width)
            )
            coef[c, pl.ds(slot * rows, rows)] = jnp.where(inside(slot), value, 0.0)

    for slot in (1, 0, 2):
        ok = row_ok(slot - 1)
        for k in range(n):
            ps = lax.rem(p + k, n)
            mine = k == 0 and slot == 1
            if not mine:
                view = rx.at[ps, slot, pl.ds(0, count)]
                await_copy(ok, view, r_main.at[ps, slot])
            await_copy(ok & out_ok, rh.at[ps, slot], r_rim.at[ps, slot])

            def got(m):
                return tx[p, m] if mine else rx[ps, slot, m]

            rim = rh[ps, slot]
            low = jnp.where(first, rim, got(0))
            high = jnp.where(first, got(0), rim)
            if n > 2:
                high = jnp.where(first | last, high, got(planes - 1))
            for q in range(pl_local):
                m, s = q // n, q % n
                value = jnp.where(
                    low_side, roll(low, -q * RIM),
                    jnp.where(
                        high_side, roll(high, RIM + width - q * RIM),
                        roll(got(1 + m), RIM - s * width),
                    ),
                )
                ext[2 + ps * pl_local + q, pl.ds(slot * rows, rows)] = jnp.where(
                    inside(slot), value, 0.0
                )

    def section(src, dst, r0, size, combine):
        e0, e1, e2, nu = (coef[c, pl.ds(r0, size)] for c in range(4))

        def body(a, carry):
            def at(k, d=0):
                return src[a + 2 + k, pl.ds(r0 + d, size)]

            c = at(0)
            a1, b1, a2, b2 = at(1), at(-1), at(2), at(-2)
            u1, d1, u2, d2 = at(0, 1), at(0, -1), at(0, 2), at(0, -2)
            g1, h1 = pltpu.roll(c, LANES - 1, 1), pltpu.roll(c, 1, 1)
            g2, h2 = pltpu.roll(c, LANES - 2, 1), pltpu.roll(c, 2, 1)
            change = e0 * (8.0 * (a1 - b1) - (a2 - b2))
            change += e1 * (8.0 * (u1 - d1) - (u2 - d2))
            change += e2 * (8.0 * (g1 - h1) - (g2 - h2))
            change += nu * (((a1 + b1) + (u1 + d1)) + (g1 + h1) - 6.0 * c)
            dst[a + 2, pl.ds(r0, size)] = combine(a, c + change)
            return carry

        lax.fori_loop(0, nphi, body, 0)

    def wrap(ref, r0, size):
        at = pl.ds(r0, size)
        ref[pl.ds(0, 2), at] = ref[pl.ds(nphi, 2), at]
        ref[pl.ds(nphi + 2, 2), at] = ref[pl.ds(2, 2), at]

    def rotated(r0):
        value = one[pl.ds(2, nphi), pl.ds(r0, 8)]
        turns = coef[4, pl.ds(r0, 8)].astype(jnp.int32)
        span = 1
        while span < nphi:
            moved = jnp.concatenate([value[nphi - span :], value[: nphi - span]], axis=0)
            value = jnp.where(((turns & span) != 0)[None], moved, value)
            span *= 2
        return value

    for step, (ra, rb, rd) in enumerate((((4, 40), (8, 32), (8, 32)), ((12, 24), (12, 24), (16, 16)))):
        wrap(ext, *ra)
        section(ext, one, *ra, lambda a, v: v)
        wrap(one, *ra)
        section(
            one, two, *rb, lambda a, v: 0.75 * ext[a + 2, pl.ds(rb[0], rb[1])] + 0.25 * v
        )
        wrap(two, *rb)
        section(
            two, one, *rd,
            lambda a, v: ext[a + 2, pl.ds(rd[0], rd[1])] * (1.0 / 3.0) + (2.0 / 3.0) * v,
        )
        for r0 in range(rd[0], rd[0] + rd[1], 8):
            ext[pl.ds(2, nphi), pl.ds(r0, 8)] = rotated(r0)

    def out_copy(k):
        t = lax.rem(p + k, n)
        return pltpu.make_async_remote_copy(
            src_ref=txo.at[k], dst_ref=rxo.at[p],
            send_sem=s_out.at[k], recv_sem=r_out.at[p],
            device_id=dev(t, 0, 0), device_id_type=MESH,
        )

    for k in range(1, n):
        t = lax.rem(p + k, n)
        for m in range(tiles):
            acc = None
            for s in range(n):
                part = roll(
                    ext[2 + t * pl_local + m * n + s, pl.ds(rows, rows)], s * width - RIM
                )
                acc = part if acc is None else jnp.where(lane >= s * width, part, acc)
            txo[k, m] = acc
        out_copy(k).start()

    for q in range(pl_local):
        out[q] = roll(ext[2 + p * pl_local + q, pl.ds(rows, rows)], p * width - RIM)
    for k in range(1, n):
        ps = lax.rem(p + k, n)
        await_copy(True, rxo.at[ps], r_out.at[ps])
        here = (lane >= ps * width) & (lane < (ps + 1) * width)
        for q in range(pl_local):
            m, s = q // n, q % n
            out[q] = jnp.where(here, roll(rxo[ps, m], ps * width - s * width), out[q])
    for ok, make in sends:
        @pl.when(ok)
        def _():
            make().wait_send()
    for k in range(1, n):
        out_copy(k).wait_send()


def local(sizes, density, drift_speed, viscosity, offsets):
    n = sizes[0]
    pl_local, rows, lanes = density.shape
    tiles = pl_local // n
    planes = tiles + 2
    nphi = n * pl_local
    f32 = jnp.float32
    block = (rows, lanes)
    deep = (3 * rows, lanes)
    vmem = pl.BlockSpec(memory_space=pltpu.VMEM)
    dma = pltpu.SemaphoreType.DMA
    return pl.pallas_call(
        functools.partial(kernel, sizes),
        out_shape=jax.ShapeDtypeStruct(density.shape, f32),
        in_specs=[vmem, vmem, vmem, pl.BlockSpec(memory_space=pltpu.SMEM)],
        out_specs=vmem,
        scratch_shapes=[
            pltpu.VMEM((n, planes) + block, f32),
            pltpu.VMEM((n, 3, planes) + block, f32),
            pltpu.VMEM((n, 3) + block, f32),
            pltpu.VMEM((5,) + block, f32),
            pltpu.VMEM((3, 5) + block, f32),
            pltpu.VMEM((2,) + block, f32),
            pltpu.VMEM((3,) + block, f32),
            pltpu.VMEM((nphi + 4,) + deep, f32),
            pltpu.VMEM((nphi + 4,) + deep, f32),
            pltpu.VMEM((nphi + 4,) + deep, f32),
            pltpu.VMEM((5,) + deep, f32),
            pltpu.VMEM((n, tiles) + block, f32),
            pltpu.VMEM((n, tiles) + block, f32),
            dma((n, 3)), dma((n, 3)), dma((2, 3)), dma((n, 3)), dma((3,)), dma((3,)),
            dma((3,)), dma((3,)), dma((n,)), dma((n,)),
        ],
        compiler_params=pltpu.CompilerParams(
            collective_id=0, has_side_effects=True, vmem_limit_bytes=32 * 1024 * 1024
        ),
    )(density, drift_speed, viscosity, offsets)


def solution(mesh):
    sizes = (mesh.shape["phi"], mesh.shape["row"], mesh.shape["gz"])
    in_specs = (P("phi", "row", "gz"), P(None, "row", "gz"), P("row", "gz"), P("row"))
    return jax.shard_map(
        functools.partial(local, sizes), mesh=mesh, in_specs=in_specs,
        out_specs=P("phi", "row", "gz"), check_vma=False,
    )
```

time: 77.1 us -> 27 us (0.35)
  waiting for transfers between devices: 39.4 us -> 0 us
  starting transfers between devices: 26.9 us -> 0 us
  Pallas kernels: 0 us -> 23.2 us
  other arithmetic: 8.93 us -> 0 us
  local copies, waits for them, and re-layouts: 1.21 us -> 3.56 us
    ppermute x20 -> x0, waiting for transfers between devices: 39.4 us -> none  [the longest x8 20.4 us: padded_2(): lax.ppermute(lax.slice_in_dim(block, block.shape[dim] - width, None, axis...]
    ppermute x20 -> x0, starting transfers between devices: 26.9 us -> none  [the longest x8 14.2 us: padded_2(): lax.ppermute(lax.slice_in_dim(block, 0, width, axis=dim), axis, backward)]
    pallas_call x0 -> x1, Pallas kernels: none -> 23.2 us  [local(): pl.pallas_call(functools.partial(kernel, sizes), out_shape=jax.ShapeDtype...]
    select_n x14 -> x0, other arithmetic: 6.81 us -> none  [the longest x6 5.54 us: zero_outside(): return jnp.where(inside[None], values, 0.0)]
    unnamed x10 -> x9, local copies, waits for them, and re-layouts: 0.56 us -> 3.56 us
    concatenate x8 -> x0, other arithmetic: 1.03 us -> none  [the longest x1 0.77 us: local(): coefficients = jnp.concatenate([drift_speed, viscosity[None]], axis=0)]
  transfers between devices with their start and end apart: 20 -> 0, of which waited for: 14 -> 0; matrix products, arithmetic and copies ran while one was open for 1% -> 0% of each run, Pallas kernels for 0% -> 0%
where the time goes in v1:
time: 27 us; the launch traced here: 26.8 us
  Pallas kernels  23.2 us (86%)
  local copies, waits for them, and re-layouts  3.56 us (13%)
    pallas_call x1, Pallas kernels, local(): pl.pallas_call(functools.partial(kernel, sizes), out_shape=jax.ShapeDtype...  23.2 us
    unnamed x9, local copies, waits for them, and re-layouts  3.56 us

profile of v1, /device:TPU:0, one launch (start us, length us, event | category | flops | bytes accessed | tf_op | source)
XLA Modules:
  0.0 26.8 jit_solution(16433618097748014350)
XLA Ops:
  0.0 0.0 copy-start
  0.0 0.8 %copy-done = f32[8,16,128]{2,1,0:T(8,128)S(1)} copy-done((f32[8,16,128]{2,1,0:T(8,128)S(1)}, f32[8,16,128]{2,1,0:T(8,128)}, u32[]{:S(2)}) %copy-start) | copy-done | bytes 65560
  0.8 0.0 copy-start.1
  0.8 0.7 %copy-done.1 = f32[3,16,128]{2,1,0:T(8,128)S(1)} copy-done((f32[3,16,128]{2,1,0:T(8,128)S(1)}, f32[3,16,128]{2,1,0:T(8,128)}, u32[]{:S(2)}) %copy-start.1) | copy-done | bytes 24600
  1.6 0.0 copy-start.2
  1.6 0.7 %copy-done.2 = f32[16,128]{1,0:T(8,128)S(1)} copy-done((f32[16,128]{1,0:T(8,128)S(1)}, f32[16,128]{1,0:T(8,128)}, u32[]{:S(2)}) %copy-start.2) | copy-done | bytes 8216
  2.3 0.0 copy-start.3
  2.3 0.7 %copy-done.3 = s32[16]{0:T(128)S(1)} copy-done((s32[16]{0:T(128)S(1)}, s32[16]{0:T(128)}, u32[]{:S(2)}) %copy-start.3) | copy-done | bytes 88
  2.9 23.2 %shard_map.46 = f32[8,16,128]{2,1,0:T(8,128)S(1)} custom-call(f32[8,16,128]{2,1,0:T(8,128)S(1)} %copy-done, f32[3,16,128]{2,1,0:T(8,128)S(1)} %copy-done.1, f32[16,128]{1,0:T(8,128)S(1)} %copy-done.2, s32[16]{0:T(128)S(1)} %copy-done.3), custom_call_target="tpu_custom_call" | custom-call | tf_op jit(solution)/shard_map/pallas_call | solution.py:314
  26.2 0.6 %copy.6 = f32[8,16,128]{2,1,0:T(8,128)} copy(f32[8,16,128]{2,1,0:T(8,128)S(1)} %shard_map.46) | data formatting | bytes 131072
Async XLA Ops:
  0.0 0.8 %copy-start = (f32[8,16,128]{2,1,0:T(8,128)S(1)}, f32[8,16,128]{2,1,0:T(8,128)}, u32[]{:S(2)}) copy-start(f32[8,16,128]{2,1,0:T(8,128)} %dens.1) | copy-start | bytes 196612
  0.8 0.7 %copy-start.1 = (f32[3,16,128]{2,1,0:T(8,128)S(1)}, f32[3,16,128]{2,1,0:T(8,128)}, u32[]{:S(2)}) copy-start(f32[3,16,128]{2,1,0:T(8,128)} %drift.1) | copy-start | bytes 73732
  1.6 0.7 %copy-start.2 = (f32[16,128]{1,0:T(8,128)S(1)}, f32[16,128]{1,0:T(8,128)}, u32[]{:S(2)}) copy-start(f32[16,128]{1,0:T(8,128)} %visc.1) | copy-start | bytes 24580
  2.3 0.7 %copy-start.3 = (s32[16]{0:T(128)S(1)}, s32[16]{0:T(128)}, u32[]{:S(2)}) copy-start(s32[16]{0:T(128)} %offs.1) | copy-start | bytes 196

commit v2 on v1

--- a/solution.py
+++ b/solution.py
@@ -14,11 +14,19 @@
 
 
 def kernel(
-    sizes, dens, drift, visc, offs, out,
+    sizes, dens_in, drift_in, visc_in, offs_in, out, dens, drift, visc, offs, s_in,
     tx, rx, rh, cx, rc, ch, rch, ext, one, two, coef, txo, rxo,
     s_main, r_main, s_rim, r_rim, s_coef, r_coef, s_crim, r_crim, s_out, r_out,
 ):
     n, nrow, ngz = sizes
+    loads = [
+        pltpu.make_async_copy(src, dst, s_in.at[at])
+        for at, (src, dst) in enumerate(
+            ((offs_in, offs), (drift_in, drift), (visc_in, visc), (dens_in, dens))
+        )
+    ]
+    for load in loads:
+        load.start()
     pl_local, rows, _ = dens.shape
     width = LANES // n
     tiles = pl_local // n
@@ -62,6 +70,8 @@
             return x if by == 0 else pltpu.roll(x, by, 1)
         return pltpu.roll(x, lax.rem(by + 4 * LANES, LANES), 1)
 
+    for load in loads[:3]:
+        load.wait()
     for c in range(3):
         cx[c] = drift[c] * (-1.0 / 12.0)
     cx[3] = visc[...]
@@ -77,6 +87,7 @@
     ch[0] = low
     ch[1] = high
 
+    loads[3].wait()
     for t in range(n):
         for m in range(tiles):
             acc = None
@@ -231,7 +242,7 @@
             dst[a + 2, pl.ds(r0, size)] = combine(a, c + change)
             return carry
 
-        lax.fori_loop(0, nphi, body, 0)
+        lax.fori_loop(0, nphi, body, 0, unroll=16 if nphi % 16 == 0 else 1)
 
     def wrap(ref, r0, size):
         at = pl.ds(r0, size)
@@ -314,9 +325,14 @@
     return pl.pallas_call(
         functools.partial(kernel, sizes),
         out_shape=jax.ShapeDtypeStruct(density.shape, f32),
-        in_specs=[vmem, vmem, vmem, pl.BlockSpec(memory_space=pltpu.SMEM)],
+        in_specs=[pl.BlockSpec(memory_space=pltpu.HBM)] * 4,
         out_specs=vmem,
         scratch_shapes=[
+            pltpu.VMEM(density.shape, f32),
+            pltpu.VMEM(drift_speed.shape, f32),
+            pltpu.VMEM(viscosity.shape, f32),
+            pltpu.SMEM(offsets.shape, jnp.int32),
+            dma((4,)),
             pltpu.VMEM((n, planes) + block, f32),
             pltpu.VMEM((n, 3, planes) + block, f32),
             pltpu.VMEM((n, 3) + block, f32),

time: 27 us -> 19.5 us (0.72)
  Pallas kernels: 23.2 us -> 15.7 us
    pallas_call x1, Pallas kernels: 23.2 us -> 15.7 us  [local(): pl.pallas_call(functools.partial(kernel, sizes), out_shape=jax.ShapeDtype...]
where the time goes in v2:
time: 19.5 us; the launch traced here: 19.3 us
  Pallas kernels  15.7 us (81%)
  local copies, waits for them, and re-layouts  3.56 us (18%)
    pallas_call x1, Pallas kernels, local(): pl.pallas_call(functools.partial(kernel, sizes), out_shape=jax.ShapeDtype...  15.7 us
    unnamed x9, local copies, waits for them, and re-layouts  3.56 us

profile of v2, /device:TPU:0, one launch (start us, length us, event | category | flops | bytes accessed | tf_op | source)
XLA Modules:
  0.0 19.3 jit_solution(10525651982458550015)
XLA Ops:
  0.0 0.0 copy-start
  0.0 0.8 %copy-done = f32[8,16,128]{2,1,0:T(8,128)S(1)} copy-done((f32[8,16,128]{2,1,0:T(8,128)S(1)}, f32[8,16,128]{2,1,0:T(8,128)}, u32[]{:S(2)}) %copy-start) | copy-done | bytes 65560
  0.8 0.0 copy-start.1
  0.8 0.7 %copy-done.1 = f32[3,16,128]{2,1,0:T(8,128)S(1)} copy-done((f32[3,16,128]{2,1,0:T(8,128)S(1)}, f32[3,16,128]{2,1,0:T(8,128)}, u32[]{:S(2)}) %copy-start.1) | copy-done | bytes 24600
  1.6 0.0 copy-start.2
  1.6 0.7 %copy-done.2 = f32[16,128]{1,0:T(8,128)S(1)} copy-done((f32[16,128]{1,0:T(8,128)S(1)}, f32[16,128]{1,0:T(8,128)}, u32[]{:S(2)}) %copy-start.2) | copy-done | bytes 8216
  2.3 0.0 copy-start.3
  2.3 0.7 %copy-done.3 = s32[16]{0:T(128)S(1)} copy-done((s32[16]{0:T(128)S(1)}, s32[16]{0:T(128)}, u32[]{:S(2)}) %copy-start.3) | copy-done | bytes 88
  2.9 15.7 %shard_map.46 = f32[8,16,128]{2,1,0:T(8,128)S(1)} custom-call(f32[8,16,128]{2,1,0:T(8,128)S(1)} %copy-done, f32[3,16,128]{2,1,0:T(8,128)S(1)} %copy-done.1, f32[16,128]{1,0:T(8,128)S(1)} %copy-done.2, s32[16]{0:T(128)S(1)} %copy-done.3), custom_call_target="tpu_custom_call" | custom-call | tf_op jit(solution)/shard_map/pallas_call | solution.py:325
  18.6 0.6 %copy.6 = f32[8,16,128]{2,1,0:T(8,128)} copy(f32[8,16,128]{2,1,0:T(8,128)S(1)} %shard_map.46) | data formatting | bytes 131072
Async XLA Ops:
  0.0 0.8 %copy-start = (f32[8,16,128]{2,1,0:T(8,128)S(1)}, f32[8,16,128]{2,1,0:T(8,128)}, u32[]{:S(2)}) copy-start(f32[8,16,128]{2,1,0:T(8,128)} %dens_in.1) | copy-start | bytes 196612
  0.8 0.7 %copy-start.1 = (f32[3,16,128]{2,1,0:T(8,128)S(1)}, f32[3,16,128]{2,1,0:T(8,128)}, u32[]{:S(2)}) copy-start(f32[3,16,128]{2,1,0:T(8,128)} %drift_in.1) | copy-start | bytes 73732
  1.6 0.7 %copy-start.2 = (f32[16,128]{1,0:T(8,128)S(1)}, f32[16,128]{1,0:T(8,128)}, u32[]{:S(2)}) copy-start(f32[16,128]{1,0:T(8,128)} %visc_in.1) | copy-start | bytes 24580
  2.3 0.7 %copy-start.3 = (s32[16]{0:T(128)S(1)}, s32[16]{0:T(128)}, u32[]{:S(2)}) copy-start(s32[16]{0:T(128)} %offs_in.1) | copy-start | bytes 196

commit v3 on v2

--- a/solution.py
+++ b/solution.py
@@ -350,7 +350,7 @@
             dma((3,)), dma((3,)), dma((n,)), dma((n,)),
         ],
         compiler_params=pltpu.CompilerParams(
-            collective_id=0, has_side_effects=True, vmem_limit_bytes=32 * 1024 * 1024
+            collective_id=0, has_side_effects=True, vmem_limit_bytes=60 * 1024 * 1024
         ),
     )(density, drift_speed, viscosity, offsets)
 

time: 19.5 us -> 17.8 us (0.913)
  local copies, waits for them, and re-layouts: 3.56 us -> 1.47 us
  Pallas kernels: 15.7 us -> 16.1 us
    unnamed x9 -> x1, local copies, waits for them, and re-layouts: 3.56 us -> 1.47 us
    pallas_call x1, Pallas kernels: 15.7 us -> 16.1 us  [local(): pl.pallas_call(functools.partial(kernel, sizes), out_shape=jax.ShapeDtype...]
where the time goes in v3:
time: 17.8 us; the launch traced here: 17.6 us
  Pallas kernels  16.1 us (90%)
  local copies, waits for them, and re-layouts  1.47 us (8%)
    pallas_call x1, Pallas kernels, local(): pl.pallas_call(functools.partial(kernel, sizes), out_shape=jax.ShapeDtype...  16.1 us
    unnamed x1, local copies, waits for them, and re-layouts  1.47 us

profile of v3, /device:TPU:0, one launch (start us, length us, event | category | flops | bytes accessed | tf_op | source)
XLA Modules:
  0.0 17.6 jit_solution(3041168396417912963)
XLA Ops:
  0.0 16.1 %shard_map.46 = f32[8,16,128]{2,1,0:T(8,128)} custom-call(f32[8,16,128]{2,1,0:T(8,128)} %dens_in.1, f32[3,16,128]{2,1,0:T(8,128)} %drift_in.1, f32[16,128]{1,0:T(8,128)} %visc_in.1, s32[16]{0:T(128)} %offs_in.1), custom_call_target="tpu_custom_call" | custom-call | tf_op jit(solution)/shard_map/pallas_call | solution.py:325
  16.1 1.5 %copy.6 = f32[8,16,128]{2,1,0:T(8,128)} copy(f32[8,16,128]{2,1,0:T(8,128)} %shard_map.46) | data formatting | bytes 131072

commit v4 on v3

--- a/solution.py
+++ b/solution.py
@@ -146,10 +146,6 @@
         )
 
     sends = []
-    for k in list(range(1, n)) + [0]:
-        for d in (-1, 1, 0):
-            if k or d:
-                sends.append((row_ok(d), functools.partial(main_copy, k, d)))
     for d in (-1, 1):
         sends.append((row_ok(d), functools.partial(coef_copy, d)))
     for d in (-1, 1, 0):
@@ -157,6 +153,10 @@
         sends.append((row_ok(d) & has_down, functools.partial(rim_copy, 1, d)))
         sends.append((row_ok(d) & has_up & first, functools.partial(crim_copy, 0, d)))
         sends.append((row_ok(d) & has_down & last, functools.partial(crim_copy, 1, d)))
+    for k in list(range(1, n)) + [0]:
+        for d in (-1, 1, 0):
+            if k or d:
+                sends.append((row_ok(d), functools.partial(main_copy, k, d)))
     for ok, make in sends:
         @pl.when(ok)
         def _():

time: 17.8 us -> 17.1 us (0.961)
  Pallas kernels: 16.1 us -> 15.4 us
    pallas_call x1, Pallas kernels: 16.1 us -> 15.4 us  [local(): pl.pallas_call(functools.partial(kernel, sizes), out_shape=jax.ShapeDtype...]
where the time goes in v4:
time: 17.1 us; the launch traced here: 16.9 us
  Pallas kernels  15.4 us (90%)
  local copies, waits for them, and re-layouts  1.47 us (9%)
    pallas_call x1, Pallas kernels, local(): pl.pallas_call(functools.partial(kernel, sizes), out_shape=jax.ShapeDtype...  15.4 us
    unnamed x1, local copies, waits for them, and re-layouts  1.47 us

profile of v4, /device:TPU:0, one launch (start us, length us, event | category | flops | bytes accessed | tf_op | source)
XLA Modules:
  0.0 16.9 jit_solution(14885861205717105059)
XLA Ops:
  0.0 15.4 %shard_map.46 = f32[8,16,128]{2,1,0:T(8,128)} custom-call(f32[8,16,128]{2,1,0:T(8,128)} %dens_in.1, f32[3,16,128]{2,1,0:T(8,128)} %drift_in.1, f32[16,128]{1,0:T(8,128)} %visc_in.1, s32[16]{0:T(128)} %offs_in.1), custom_call_target="tpu_custom_call" | custom-call | tf_op jit(solution)/shard_map/pallas_call | solution.py:325
  15.4 1.5 %copy.6 = f32[8,16,128]{2,1,0:T(8,128)} copy(f32[8,16,128]{2,1,0:T(8,128)} %shard_map.46) | data formatting | bytes 131072
